TPU v7x, 128 devices: a whole 4x4x4 slice. The times are simulated.
128 devices in a mesh: rows: 16 (over x, z), cols: 8 (over y, core).
Axes of the slice: x: 4, y: 4, z: 4, core: 2. Of those that a mesh axis runs over, the one named last changes fastest.
Arguments:
- counts: int32 [2048, 512, 512], P(('rows', 'cols')), may hold values from 0 to 1024, as said below
- shard_rows: int32 [2048], P(('rows', 'cols')), may hold values from 0 to 255, as said below
- shard_cols: int32 [2048], P(('rows', 'cols')), may hold values from 0 to 255, as said below
- listed: int32 [128], P(('rows', 'cols')), may hold values from 2 to 16, as said below
- row_embed: float32 [131072, 256], P(('rows', 'cols')), may hold values from -1.5 to 1.5
- row_accum: float32 [131072, 256], P(('rows', 'cols')), may hold values from 300 to 10000
- row_offset: bfloat16 [131072], P(('rows', 'cols')), may hold values from -3 to -1
- col_embed: float32 [131072, 256], P(('rows', 'cols')), may hold values from -1.5 to 1.5
- col_accum: float32 [131072, 256], P(('rows', 'cols')), may hold values from 300 to 10000
- col_offset: bfloat16 [131072], P(('rows', 'cols')), may hold values from -3 to -1
Outputs:
- row_trained: float32 [131072, 256], P(('rows', 'cols'))
- col_trained: float32 [131072, 256], P(('rows', 'cols'))
Inputs may be any that keep to these rules, and one draw needn't show every extreme that they name: `shard_rows`: entry q belongs to holder h = q // 16, the device at rows index h // 8 and cols index h % 8. Row block g is owned by device g // 2 in the same order. The row block of a listed entry is owned by a device with its holder's cols index; the listed entries of one holder use at most 1 different row blocks of any one owner, and in some holder exactly 1 of each of the 16 owners with its cols index. `shard_cols`: column block c is owned by device c // 2. The column block of a listed entry is owned by a device with its holder's rows index. No holder lists the same pair of blocks twice. The listed entries of holder h are its first listed[h] ones; its other entries and their counts take no part. `counts`: zero where the pair of items never occurs together.
All inputs are finite; a program needn't handle non-finite values.
Results may differ from a plain program's by a relative error of at most 0.0014.
Values may be sent and summed in bfloat16 or wider, within the bound.
A program may use at most 192 MiB of HBM per device.

v0:
```python
import jax
import jax.numpy as jnp
from jax import lax
from jax.sharding import PartitionSpec as P

learning_rate = 0.5
conf_base = 0.1
conf_scale = 0.25
shard_group = 4


def slopes(cell_counts, scores, row_shift, col_shift):
    floored = jnp.maximum(cell_counts, 1).astype(jnp.float32)
    pointwise = jnp.log(floored) + row_shift[:, :, None] + col_shift[:, None, :]
    weight = conf_base + conf_scale * jnp.sqrt(floored)
    return jnp.where(
        cell_counts > 0, weight * (scores - pointwise), jax.nn.sigmoid(scores - pointwise)
    )


def process(
    count_tiles, live_count, row_pool, row_shifts, row_index, col_pool, col_shifts, col_index
):
    turns = count_tiles.shape[0] // shard_group

    def one_turn(turn_index, totals):
        row_grad, col_grad = totals
        first = turn_index * shard_group
        tile_group = lax.dynamic_slice_in_dim(count_tiles, first, shard_group, 0)
        row_slots = lax.dynamic_slice_in_dim(row_index, first, shard_group, 0)
        col_slots = lax.dynamic_slice_in_dim(col_index, first, shard_group, 0)
        row_vectors = jnp.take(row_pool, row_slots, axis=0)
        col_vectors = jnp.take(col_pool, col_slots, axis=0)
        scores = jnp.einsum(
            "sbd,sed->sbe", row_vectors, col_vectors, preferred_element_type=jnp.float32
        )
        row_shift = jnp.take(row_shifts, row_slots, axis=0).astype(jnp.float32)
        col_shift = jnp.take(col_shifts, col_slots, axis=0).astype(jnp.float32)
        slope_full = slopes(tile_group, scores, row_shift, col_shift)
        in_list = first + jnp.arange(shard_group, dtype=jnp.int32) < live_count
        slope_full = jnp.where(in_list[:, None, None], slope_full, jnp.zeros_like(slope_full))
        slope_half = slope_full.astype(jnp.bfloat16)
        row_terms = jnp.einsum(
            "sbe,sed->sbd", slope_half, col_vectors, preferred_element_type=jnp.float32
        )
        col_terms = jnp.einsum(
            "sbe,sbd->sed", slope_half, row_vectors, preferred_element_type=jnp.float32
        )
        return (row_grad.at[row_slots].add(row_terms), col_grad.at[col_slots].add(col_terms))

    start = (jnp.zeros(row_pool.shape, jnp.float32), jnp.zeros(col_pool.shape, jnp.float32))
    return lax.fori_loop(0, turns, one_turn, start)


def on_device(
    counts,
    shard_rows,
    shard_cols,
    listed,
    row_embed,
    row_accum,
    row_offset,
    col_embed,
    col_accum,
    col_offset,
):
    block_items = counts.shape[1]
    features = row_embed.shape[1]
    row_owned = row_embed.shape[0] // block_items
    col_owned = col_embed.shape[0] // block_items
    col_devices = lax.axis_size("cols")
    live_count = listed[0]
    row_set = shard_rows // row_owned // col_devices * row_owned + shard_rows % row_owned
    col_set = shard_cols // col_owned % col_devices * col_owned + shard_cols % col_owned
    row_half = row_embed.astype(jnp.bfloat16)
    col_half = col_embed.astype(jnp.bfloat16)
    col_pool = lax.all_gather(col_half, "cols", axis=0, tiled=True)
    col_shifts = lax.all_gather(col_offset, "cols", axis=0, tiled=True)
    row_pool = lax.all_gather(row_half, "rows", axis=0, tiled=True)
    row_shifts = lax.all_gather(row_offset, "rows", axis=0, tiled=True)
    row_pool = row_pool.reshape(-1, block_items, features)
    row_shifts = row_shifts.reshape(-1, block_items)
    row_part, col_part = process(
        counts,
        live_count,
        row_pool,
        row_shifts,
        row_set,
        col_pool.reshape(-1, block_items, features),
        col_shifts.reshape(-1, block_items),
        col_set,
    )
    row_grad = lax.psum_scatter(
        row_part.reshape(-1, features), "rows", scatter_dimension=0, tiled=True
    )
    col_grad = lax.psum_scatter(
        col_part.reshape(-1, features), "cols", scatter_dimension=0, tiled=True
    )
    row_accum = row_accum + row_grad * row_grad
    col_accum = col_accum + col_grad * col_grad
    row_embed = row_embed - learning_rate * row_grad / jnp.sqrt(row_accum)
    col_embed = col_embed - learning_rate * col_grad / jnp.sqrt(col_accum)
    return (row_embed, col_embed)


def solution(mesh):
    in_specs = (
        P(("rows", "cols"), None, None),
        P(("rows", "cols")),
        P(("rows", "cols")),
        P(("rows", "cols")),
        P(("rows", "cols"), None),
        P(("rows", "cols"), None),
        P(("rows", "cols")),
        P(("rows", "cols"), None),
        P(("rows", "cols"), None),
        P(("rows", "cols")),
    )
    out_specs = (P(("rows", "cols"), None), P(("rows", "cols"), None))
    return jax.shard_map(
        on_device, mesh=mesh, in_specs=in_specs, out_specs=out_specs, check_vma=False
    )
```

profile of v0, /device:TPU:1, one launch (start us, length us, event | category | flops | bytes accessed | tf_op | source)
XLA Modules:
  0.0 412.7 jit_solution(9346505922726020721)
XLA Ops:
  7.3 2.1 convert_element_type.43
  9.4 2.1 convert_element_type.42
  11.6 13.5 %all_gather.15 = bf16[8192]{0:T(1024)(128)(2,1)S(1)} all-gather(bf16[1024]{0:T(1024)(128)(2,1)S(1)} %copy-done.3), channel_id=1, replica_groups=mesh['rows'=16,'cols'=8] {'cols'}, dimensions={0}, use_global_device_ids=true | all-gather | bytes 18432 | tf_op jit(solution)/shard_map/all_gather | solution.py:78
  25.1 21.2 %all_gather.14 = bf16[16384]{0:T(1024)(128)(2,1)S(1)} all-gather(bf16[1024]{0:T(1024)(128)(2,1)S(1)} %copy-done.4), channel_id=1, replica_groups=mesh['rows'=16,'cols'=8] {'rows'}, dimensions={0}, use_global_device_ids=true | all-gather | bytes 34816 | tf_op jit(solution)/shard_map/all_gather | solution.py:80
  46.4 72.6 %all-gather.3.cloned.1.call-done = bf16[16384,256]{1,0:T(8,128)(2,1)} async-done(((bf16[1024,256]{1,0:T(8,128)(2,1)}), bf16[16384,256]{1,0:T(8,128)(2,1)}) %all-gather.3.cloned.1.call-update) | async-done | bytes 8388624 | tf_op jit(solution)/shard_map/all_gather | solution.py:79
  119.0 4.1 broadcast_in_dim.102
  123.2 7.7 %broadcast_in_dim.101 = f32[32,512,256]{2,1,0:T(8,128)} broadcast(f32[]{:T(128)} %constant.184.clone.1), dimensions={} | broadcast | bytes 16777220 | tf_op jit(solution)/shard_map/broadcast_in_dim | solution.py:51
  130.9 106.7 %while.15 = (s32[]{:T(128)}, f32[32,512,256]{2,1,0:T(8,128)}, f32[16,512,256]{2,1,0:T(8,128)}, s32[16]{0:T(128)S(1)}, s32[]{:T(128)}, /*index=5*/s32[16,512,512]...) while((s32[]{:T(128)}, f32[32,512,256]{2,1,0:T(8,128)}, ...), condition=%wide.region_3.4_spmd, body=%wide.region_0.3_spmd.sunk | while | flops 1629497344 | bytes 35717552 | solution.py:52
  130.9 0.7 add_compare_fusion.2
  131.5 0.1 compare_and_fusion.3
  131.6 0.6 gather_fusion
  132.2 0.1 select_convert_fusion.6
  132.3 0.6 gather_fusion.1
  132.8 0.1 select_convert_fusion.7
  132.9 4.0 gather_fusion.2
  136.9 2.8 gather_fusion.3
  139.7 5.6 %select_convert_fusion.8 = bf16[4,512,512]{2,1,0:T(8,128)(2,1)S(1)} fusion(s32[16,512,512]{2,1,0:T(8,128)} %get-tuple-element.329, s32[]{:T(128)S(6)} %select_n.171, f32[4,512]{1,0:T(4,128)S(1)} %select_convert_fusion.6, f32[4,512]{1,0:T(4,128)S(1)} %select_convert_fusion.7, pred[4]{0:T(512)(128)(4,1)S(1)} %add_compare_fusion.2, ...), kind=kOutput, calls=%fused_computation.6.clone.1 | convolution fusion | flops 553648128 | bytes 8405008 | tf_op jit(solution)/shard_map/while/body/eval_jaxpr/sbd,sed->sbe/dot_general | solution.py:34
  145.3 2.2 fusion.18
  147.5 0.8 fusion.17
  148.3 4.9 %scatter_fusion.1 = f32[16,512,256]{2,1,0:T(8,128)} fusion(f32[16,512,256]{2,1,0:T(8,128)} %get-tuple-element.311, s32[4]{0:T(128)S(1)} %get-tuple-element.291, f32[4,512,256]{2,1,0:T(8,128)} %fusion.18), kind=kCustom, calls=%fused_computation.5.clone.1 | custom fusion | flops 524288 | bytes 6291472 | tf_op jit(solution)/shard_map/while/body/eval_jaxpr/scatter-add | solution.py:49
  153.2 4.2 %scatter_fusion = f32[32,512,256]{2,1,0:T(8,128)} fusion(f32[32,512,256]{2,1,0:T(8,128)} %get-tuple-element.310, s32[4]{0:T(128)S(1)} %get-tuple-element.290, f32[4,512,256]{2,1,0:T(8,128)S(1)} %fusion.17), kind=kCustom, calls=%fused_computation.4.clone.1 | custom fusion | flops 524288 | bytes 6291472 | tf_op jit(solution)/shard_map/while/body/eval_jaxpr/scatter-add | solution.py:49
  157.5 0.7 add_compare_fusion.2
  158.1 0.1 compare_and_fusion.3
  158.2 0.6 gather_fusion
  158.8 0.1 select_convert_fusion.6
  158.9 0.6 gather_fusion.1
  159.5 0.1 select_convert_fusion.7
  159.5 4.0 gather_fusion.2
  163.5 2.8 gather_fusion.3
  166.3 5.6 %select_convert_fusion.8 = bf16[4,512,512]{2,1,0:T(8,128)(2,1)S(1)} fusion(s32[16,512,512]{2,1,0:T(8,128)} %get-tuple-element.329, s32[]{:T(128)S(6)} %select_n.171, f32[4,512]{1,0:T(4,128)S(1)} %select_convert_fusion.6, f32[4,512]{1,0:T(4,128)S(1)} %select_convert_fusion.7, pred[4]{0:T(512)(128)(4,1)S(1)} %add_compare_fusion.2, ...), kind=kOutput, calls=%fused_computation.6.clone.1 | convolution fusion | flops 553648128 | bytes 8405008 | tf_op jit(solution)/shard_map/while/body/eval_jaxpr/sbd,sed->sbe/dot_general | solution.py:34
  171.9 2.2 fusion.18
  174.1 0.8 fusion.17
  174.9 5.0 %scatter_fusion.1 = f32[16,512,256]{2,1,0:T(8,128)} fusion(f32[16,512,256]{2,1,0:T(8,128)} %get-tuple-element.311, s32[4]{0:T(128)S(1)} %get-tuple-element.291, f32[4,512,256]{2,1,0:T(8,128)} %fusion.18), kind=kCustom, calls=%fused_computation.5.clone.1 | custom fusion | flops 524288 | bytes 6291472 | tf_op jit(solution)/shard_map/while/body/eval_jaxpr/scatter-add | solution.py:49
  179.9 4.2 %scatter_fusion = f32[32,512,256]{2,1,0:T(8,128)} fusion(f32[32,512,256]{2,1,0:T(8,128)} %get-tuple-element.310, s32[4]{0:T(128)S(1)} %get-tuple-element.290, f32[4,512,256]{2,1,0:T(8,128)S(1)} %fusion.17), kind=kCustom, calls=%fused_computation.4.clone.1 | custom fusion | flops 524288 | bytes 6291472 | tf_op jit(solution)/shard_map/while/body/eval_jaxpr/scatter-add | solution.py:49
  184.2 0.7 add_compare_fusion.2
  184.8 0.1 compare_and_fusion.3
  184.9 0.6 gather_fusion
  185.5 0.1 select_convert_fusion.6
  185.6 0.6 gather_fusion.1
  186.2 0.1 select_convert_fusion.7
  186.2 4.0 gather_fusion.2
  190.2 2.8 gather_fusion.3
  193.1 5.6 %select_convert_fusion.8 = bf16[4,512,512]{2,1,0:T(8,128)(2,1)S(1)} fusion(s32[16,512,512]{2,1,0:T(8,128)} %get-tuple-element.329, s32[]{:T(128)S(6)} %select_n.171, f32[4,512]{1,0:T(4,128)S(1)} %select_convert_fusion.6, f32[4,512]{1,0:T(4,128)S(1)} %select_convert_fusion.7, pred[4]{0:T(512)(128)(4,1)S(1)} %add_compare_fusion.2, ...), kind=kOutput, calls=%fused_computation.6.clone.1 | convolution fusion | flops 553648128 | bytes 8405008 | tf_op jit(solution)/shard_map/while/body/eval_jaxpr/sbd,sed->sbe/dot_general | solution.py:34
  198.6 2.2 fusion.18
  200.9 0.8 fusion.17
  201.6 5.0 %scatter_fusion.1 = f32[16,512,256]{2,1,0:T(8,128)} fusion(f32[16,512,256]{2,1,0:T(8,128)} %get-tuple-element.311, s32[4]{0:T(128)S(1)} %get-tuple-element.291, f32[4,512,256]{2,1,0:T(8,128)} %fusion.18), kind=kCustom, calls=%fused_computation.5.clone.1 | custom fusion | flops 524288 | bytes 6291472 | tf_op jit(solution)/shard_map/while/body/eval_jaxpr/scatter-add | solution.py:49
  206.6 4.3 %scatter_fusion = f32[32,512,256]{2,1,0:T(8,128)} fusion(f32[32,512,256]{2,1,0:T(8,128)} %get-tuple-element.310, s32[4]{0:T(128)S(1)} %get-tuple-element.290, f32[4,512,256]{2,1,0:T(8,128)S(1)} %fusion.17), kind=kCustom, calls=%fused_computation.4.clone.1 | custom fusion | flops 524288 | bytes 6291472 | tf_op jit(solution)/shard_map/while/body/eval_jaxpr/scatter-add | solution.py:49
  210.9 0.7 add_compare_fusion.2
  211.6 0.1 compare_and_fusion.3
  211.7 0.6 gather_fusion
  212.3 0.1 select_convert_fusion.6
  212.4 0.6 gather_fusion.1
  213.0 4.0 gather_fusion.2
  217.0 2.8 gather_fusion.3
  219.8 5.6 %select_convert_fusion.8 = bf16[4,512,512]{2,1,0:T(8,128)(2,1)S(1)} fusion(s32[16,512,512]{2,1,0:T(8,128)} %get-tuple-element.329, s32[]{:T(128)S(6)} %select_n.171, f32[4,512]{1,0:T(4,128)S(1)} %select_convert_fusion.6, f32[4,512]{1,0:T(4,128)S(1)} %select_convert_fusion.7, pred[4]{0:T(512)(128)(4,1)S(1)} %add_compare_fusion.2, ...), kind=kOutput, calls=%fused_computation.6.clone.1 | convolution fusion | flops 553648128 | bytes 8405008 | tf_op jit(solution)/shard_map/while/body/eval_jaxpr/sbd,sed->sbe/dot_general | solution.py:34
  225.4 2.2 fusion.18
  227.6 0.8 fusion.17
  228.4 5.0 %scatter_fusion.1 = f32[16,512,256]{2,1,0:T(8,128)} fusion(f32[16,512,256]{2,1,0:T(8,128)} %get-tuple-element.311, s32[4]{0:T(128)S(1)} %get-tuple-element.291, f32[4,512,256]{2,1,0:T(8,128)} %fusion.18), kind=kCustom, calls=%fused_computation.5.clone.1 | custom fusion | flops 524288 | bytes 6291472 | tf_op jit(solution)/shard_map/while/body/eval_jaxpr/scatter-add | solution.py:49
  233.4 4.2 %scatter_fusion = f32[32,512,256]{2,1,0:T(8,128)} fusion(f32[32,512,256]{2,1,0:T(8,128)} %get-tuple-element.310, s32[4]{0:T(128)S(1)} %get-tuple-element.290, f32[4,512,256]{2,1,0:T(8,128)S(1)} %fusion.17), kind=kCustom, calls=%fused_computation.4.clone.1 | custom fusion | flops 524288 | bytes 6291472 | tf_op jit(solution)/shard_map/while/body/eval_jaxpr/scatter-add | solution.py:49
  237.7 0.5 reduce-scatter.3.cloned.1.call-update
  238.2 51.2 %reduce-scatter.5.cloned.1.call-done = f32[1024,256]{1,0:T(8,128)} async-done(((f32[8192,256]{1,0:T(8,128)}), f32[1024,256]{1,0:T(8,128)}) %reduce-scatter.5.cloned.1.call-update) | async-done | bytes 1048592 | tf_op jit(solution)/shard_map/reduce_scatter | solution.py:96
  289.4 2.4 multiply_subtract_fusion
  291.8 111.7 %reduce-scatter.3.cloned.1.call-done = f32[1024,256]{1,0:T(8,128)} async-done(((f32[16384,256]{1,0:T(8,128)}), f32[1024,256]{1,0:T(8,128)}) %reduce-scatter.3.cloned.1.call-update) | async-done | bytes 1048592 | tf_op jit(solution)/shard_map/reduce_scatter | solution.py:93
  403.5 2.7 multiply_subtract_fusion.1
  (34 shorter events, 0.5 us)
Async XLA Ops:
  7.2 4.4 %copy-start.3 = (bf16[1024]{0:T(1024)(128)(2,1)S(1)}, bf16[1024]{0:T(1024)(128)(2,1)}, u32[]{:S(2)}) copy-start(bf16[1024]{0:T(1024)(128)(2,1)} %param.21) | copy-start | bytes 6148
  7.2 17.9 %copy-start.4 = (bf16[1024]{0:T(1024)(128)(2,1)S(1)}, bf16[1024]{0:T(1024)(128)(2,1)}, u32[]{:S(2)}) copy-start(bf16[1024]{0:T(1024)(128)(2,1)} %param.18) | copy-start | bytes 6148
  7.2 39.2 %copy-start.6 = (s32[16]{0:T(128)S(1)}, s32[16]{0:T(128)}, u32[]{:S(2)}) copy-start(s32[16]{0:T(128)} %param.14) | copy-start | bytes 196
  7.2 39.2 %copy-start.5 = (s32[16]{0:T(128)S(1)}, s32[16]{0:T(128)}, u32[]{:S(2)}) copy-start(s32[16]{0:T(128)} %param.13) | copy-start | bytes 196
  7.2 39.2 %all-gather.5.cloned.1.call-start = ((), (), s32[]{:S(2)}) async-start(), calls=%async_computation.3 | async-start | bytes 4718592 | tf_op jit(solution)/shard_map/all_gather | solution.py:77
  9.3 109.7 %all-gather.3.cloned.1.call-start = ((), (), s32[]{:S(2)}) async-start(), calls=%async_computation.2 | async-start | bytes 8912896 | tf_op jit(solution)/shard_map/all_gather | solution.py:79
  11.5 277.9 %reduce-scatter.5.cloned.1.call-start = ((), (), s32[]{:S(2)}) async-start(), calls=%async_computation.5 | async-start | bytes 9437184 | tf_op jit(solution)/shard_map/reduce_scatter | solution.py:96
  237.6 165.8 %reduce-scatter.3.cloned.1.call-start = ((), (), s32[]{:S(2)}) async-start(), calls=%async_computation.4 | async-start | bytes 17825792 | tf_op jit(solution)/shard_map/reduce_scatter | solution.py:93
  237.7 51.7 %copy-start = (f32[1024,256]{1,0:T(8,128)S(1)}, f32[1024,256]{1,0:T(8,128)}, u32[]{:S(2)}) copy-start(f32[1024,256]{1,0:T(8,128)} %param.19) | copy-start | bytes 3145732
  237.7 51.7 %copy-start.2 = (f32[1024,256]{1,0:T(8,128)S(1)}, f32[1024,256]{1,0:T(8,128)}, u32[]{:S(2)}) copy-start(f32[1024,256]{1,0:T(8,128)} %param.20) | copy-start | bytes 3145732
  238.2 165.3 %copy-start.1 = (f32[1024,256]{1,0:T(8,128)S(1)}, f32[1024,256]{1,0:T(8,128)}, u32[]{:S(2)}) copy-start(f32[1024,256]{1,0:T(8,128)} %param.16) | copy-start | bytes 3145732
Sparse Core Ops, SparseCore 0:
  10.3 35.6 all-gather.4
  48.7 70.2 all-gather.2
  237.7 51.6 reduce-scatter.4
  292.7 110.7 reduce-scatter.2
where the time goes:
time: 413 us
  waiting for transfers between devices  236 us (57%)
  other arithmetic  49.8 us (12%)
  local copies, waits for them, and re-layouts  43.6 us (11%)
  blocking collectives  34.7 us (8%)
  matrix products  34.3 us (8%)
  between operations  13.9 us (3%)
    reduce_scatter x1, waiting for transfers between devices, on_device(): lax.psum_scatter(row_part.reshape(-1, features), 'rows', scatter_dimensio...  112 us
    all_gather x1, waiting for transfers between devices, on_device(): row_pool = lax.all_gather(row_half, 'rows', axis=0, tiled=True)  72.6 us
    reduce_scatter x1, waiting for transfers between devices, on_device(): lax.psum_scatter(col_part.reshape(-1, features), 'cols', scatter_dimensio...  51.2 us
    dot_general x4, matrix products, one_turn(): jnp.einsum('sbd,sed->sbe', row_vectors, col_vectors, preferred_element_ty...  22.3 us
    all_gather x1, blocking collectives, on_device(): row_shifts = lax.all_gather(row_offset, 'rows', axis=0, tiled=True)  21.2 us
    scatter-add x4, other arithmetic, one_turn(): col_grad.at[col_slots].add(col_terms)  19.9 us
    scatter-add x4, other arithmetic, one_turn(): row_grad.at[row_slots].add(row_terms)  17 us
    gather x4, local copies, waits for them, and re-layouts, one_turn(): row_vectors = jnp.take(row_pool, row_slots, axis=0)  16 us
  transfers between devices with their start and end apart: 4, of which 3 were waited for; matrix products, arithmetic and copies ran while one was open for 1% of the time, Pallas kernels for 0%

commit v1 on v0

--- a/solution.py
+++ b/solution.py
@@ -77,7 +77,16 @@
     col_pool = lax.all_gather(col_half, "cols", axis=0, tiled=True)
     col_shifts = lax.all_gather(col_offset, "cols", axis=0, tiled=True)
     row_pool = lax.all_gather(row_half, "rows", axis=0, tiled=True)
-    row_shifts = lax.all_gather(row_offset, "rows", axis=0, tiled=True)
+    ways = lax.axis_size("rows")
+    up = [(d, (d + 1) % ways) for d in range(ways)]
+    down = [(d, (d - 1) % ways) for d in range(ways)]
+    earlier, later = ([row_offset], [row_offset])
+    for _ in range(ways // 2):
+        earlier.append(lax.ppermute(earlier[-1], "rows", up))
+    for _ in range((ways - 1) // 2):
+        later.append(lax.ppermute(later[-1], "rows", down))
+    line = jnp.concatenate([*earlier[::-1], *later[1:]], axis=0)
+    row_shifts = jnp.roll(line, (lax.axis_index("rows") - ways // 2) * row_offset.shape[0], axis=0)
     row_pool = row_pool.reshape(-1, block_items, features)
     row_shifts = row_shifts.reshape(-1, block_items)
     row_part, col_part = process(

time: 413 us -> 413 us (level)
  starting transfers between devices: 0.16 us -> 36.9 us
  waiting for transfers between devices: 236 us -> 213 us
  blocking collectives: 34.7 us -> 20.4 us
    ppermute x0 -> x15, starting transfers between devices: none -> 36.8 us  [the longest x7 34.2 us: on_device(): later.append(lax.ppermute(later[-1], 'rows', down))]
    all_gather x1, waiting for transfers between devices: 72.6 us -> 38.3 us  [on_device(): row_pool = lax.all_gather(row_half, 'rows', axis=0, tiled=True)]
    all_gather x1 -> x0, blocking collectives: 21.2 us -> none  [on_device(): row_shifts = lax.all_gather(row_offset, 'rows', axis=0, tiled=True)]
    ppermute x0 -> x15, waiting for transfers between devices: none -> 11.4 us  [the longest x8 10.8 us: on_device(): earlier.append(lax.ppermute(earlier[-1], 'rows', up))]
    all_gather x1, blocking collectives: 13.5 us -> 20.4 us  [on_device(): col_shifts = lax.all_gather(col_offset, 'cols', axis=0, tiled=True)]
  transfers between devices with their start and end apart: 4 -> 19, of which waited for: 3 -> 11; matrix products, arithmetic and copies ran while one was open for 1% -> 1% of each run, Pallas kernels for 0% -> 0%
where the time goes in v1:
time: 413 us; the launch traced here: 412 us
  waiting for transfers between devices  213 us (52%)
  other arithmetic  49.8 us (12%)
  local copies, waits for them, and re-layouts  43.9 us (11%)
  starting transfers between devices  36.9 us (9%)
  matrix products  34.3 us (8%)
  blocking collectives  20.4 us (5%)
  between operations  14 us (3%)
    reduce_scatter x1, waiting for transfers between devices, on_device(): lax.psum_scatter(row_part.reshape(-1, features), 'rows', scatter_dimensio...  112 us
    reduce_scatter x1, waiting for transfers between devices, on_device(): lax.psum_scatter(col_part.reshape(-1, features), 'cols', scatter_dimensio...  51 us
    all_gather x1, waiting for transfers between devices, on_device(): row_pool = lax.all_gather(row_half, 'rows', axis=0, tiled=True)  38.3 us
    ppermute x7, starting transfers between devices, on_device(): later.append(lax.ppermute(later[-1], 'rows', down))  34.2 us
    dot_general x4, matrix products, one_turn(): jnp.einsum('sbd,sed->sbe', row_vectors, col_vectors, preferred_element_ty...  22.3 us
    all_gather x1, blocking collectives, on_device(): col_shifts = lax.all_gather(col_offset, 'cols', axis=0, tiled=True)  20.4 us
    scatter-add x4, other arithmetic, one_turn(): col_grad.at[col_slots].add(col_terms)  19.9 us
    scatter-add x4, other arithmetic, one_turn(): row_grad.at[row_slots].add(row_terms)  17 us
  transfers between devices with their start and end apart: 19, of which 11 were waited for; matrix products, arithmetic and copies ran while one was open for 1% of the time, Pallas kernels for 0%

profile of v1, /device:TPU:1, one launch (start us, length us, event | category | flops | bytes accessed | tf_op | source)
XLA Modules:
  0.0 412.5 jit_solution(5187968068382129802)
XLA Ops:
  7.3 2.1 convert_element_type.43
  9.4 2.1 convert_element_type.42
  11.6 2.5 collective-permute-start
  14.1 5.3 %collective-permute-done = bf16[1024]{0:T(1024)(128)(2,1)S(1)} collective-permute-done((bf16[1024]{0:T(1024)(128)(2,1)S(1)}, bf16[1024]{0:T(1024)(128)(2,1)S(1)}, u32[]{:S(2)}, u32[]{:S(2)}) %collective-permute-start) | collective-permute-done | bytes 2080 | tf_op jit(solution)/shard_map/ppermute | solution.py:85
  19.4 4.8 %collective-permute-start.8 = (bf16[1024]{0:T(1024)(128)(2,1)S(1)}, bf16[1024]{0:T(1024)(128)(2,1)S(1)}, u32[]{:S(2)}, u32[]{:S(2)}) collective-permute-start(bf16[1024]{0:T(1024)(128)(2,1)S(1)} %copy-done.3), channel_id=1, source_target_pairs={{0,120},{8,0},{16,8},{24,16},{32,24},{40,32},{48,40},{56,48},{64,5... | collective-permute-start | bytes 6152 | tf_op jit(solution)/shard_map/ppermute | solution.py:87
  24.2 1.0 collective-permute-done.1
  25.1 4.8 %collective-permute-start.9 = (bf16[1024]{0:T(1024)(128)(2,1)S(1)}, bf16[1024]{0:T(1024)(128)(2,1)S(1)}, u32[]{:S(2)}, u32[]{:S(2)}) collective-permute-start(bf16[1024]{0:T(1024)(128)(2,1)S(1)} %collective-permute-done.8), channel_id=1, source_target_pairs={{0,120},{8,0},{16,8},{24,16},{32,24},{40,32},{48,40},{56,48},{64,5... | collective-permute-start | bytes 6152 | tf_op jit(solution)/shard_map/ppermute | solution.py:87
  29.9 1.0 collective-permute-done.2
  30.9 4.8 %collective-permute-start.10 = (bf16[1024]{0:T(1024)(128)(2,1)S(1)}, bf16[1024]{0:T(1024)(128)(2,1)S(1)}, u32[]{:S(2)}, u32[]{:S(2)}) collective-permute-start(bf16[1024]{0:T(1024)(128)(2,1)S(1)} %collective-permute-done.9), channel_id=1, source_target_pairs={{0,120},{8,0},{16,8},{24,16},{32,24},{40,32},{48,40},{56,48},{64,5... | collective-permute-start | bytes 6152 | tf_op jit(solution)/shard_map/ppermute | solution.py:87
  35.7 1.0 collective-permute-done.3
  36.6 4.8 %collective-permute-start.11 = (bf16[1024]{0:T(1024)(128)(2,1)S(1)}, bf16[1024]{0:T(1024)(128)(2,1)S(1)}, u32[]{:S(2)}, u32[]{:S(2)}) collective-permute-start(bf16[1024]{0:T(1024)(128)(2,1)S(1)} %collective-permute-done.10), channel_id=1, source_target_pairs={{0,120},{8,0},{16,8},{24,16},{32,24},{40,32},{48,40},{56,48},{64,5... | collective-permute-start | bytes 6152 | tf_op jit(solution)/shard_map/ppermute | solution.py:87
  41.4 1.0 collective-permute-done.4
  42.4 4.8 %collective-permute-start.12 = (bf16[1024]{0:T(1024)(128)(2,1)S(1)}, bf16[1024]{0:T(1024)(128)(2,1)S(1)}, u32[]{:S(2)}, u32[]{:S(2)}) collective-permute-start(bf16[1024]{0:T(1024)(128)(2,1)S(1)} %collective-permute-done.11), channel_id=1, source_target_pairs={{0,120},{8,0},{16,8},{24,16},{32,24},{40,32},{48,40},{56,48},{64,5... | collective-permute-start | bytes 6152 | tf_op jit(solution)/shard_map/ppermute | solution.py:87
  47.2 1.0 collective-permute-done.5
  48.2 5.0 %collective-permute-start.13 = (bf16[1024]{0:T(1024)(128)(2,1)S(1)}, bf16[1024]{0:T(1024)(128)(2,1)S(1)}, u32[]{:S(2)}, u32[]{:S(2)}) collective-permute-start(bf16[1024]{0:T(1024)(128)(2,1)S(1)} %collective-permute-done.12), channel_id=1, source_target_pairs={{0,120},{8,0},{16,8},{24,16},{32,24},{40,32},{48,40},{56,48},{64,5... | collective-permute-start | bytes 6152 | tf_op jit(solution)/shard_map/ppermute | solution.py:87
  53.2 0.7 collective-permute-done.6
  53.9 20.4 %all_gather.11 = bf16[8192]{0:T(1024)(128)(2,1)S(1)} all-gather(bf16[1024]{0:T(1024)(128)(2,1)S(1)} %copy-done.4), channel_id=1, replica_groups=mesh['rows'=16,'cols'=8] {'cols'}, dimensions={0}, use_global_device_ids=true | all-gather | bytes 18432 | tf_op jit(solution)/shard_map/all_gather | solution.py:78
  74.4 5.3 %collective-permute-start.14 = (bf16[1024]{0:T(1024)(128)(2,1)S(1)}, bf16[1024]{0:T(1024)(128)(2,1)S(1)}, u32[]{:S(2)}, u32[]{:S(2)}) collective-permute-start(bf16[1024]{0:T(1024)(128)(2,1)S(1)} %collective-permute-done.13), channel_id=1, source_target_pairs={{0,120},{8,0},{16,8},{24,16},{32,24},{40,32},{48,40},{56,48},{64,5... | collective-permute-start | bytes 6152 | tf_op jit(solution)/shard_map/ppermute | solution.py:87
  79.9 0.6 collective-permute-done.14
  80.7 38.3 %all-gather.3.cloned.1.call-done = bf16[16384,256]{1,0:T(8,128)(2,1)} async-done(((bf16[1024,256]{1,0:T(8,128)(2,1)}), bf16[16384,256]{1,0:T(8,128)(2,1)}) %all-gather.3.cloned.1.call-update) | async-done | bytes 8388624 | tf_op jit(solution)/shard_map/all_gather | solution.py:79
  119.1 4.1 broadcast_in_dim.102
  123.2 7.7 %broadcast_in_dim.101 = f32[32,512,256]{2,1,0:T(8,128)} broadcast(f32[]{:T(128)} %constant.208.clone.1), dimensions={} | broadcast | bytes 16777220 | tf_op jit(solution)/shard_map/broadcast_in_dim | solution.py:51
  130.9 106.7 %while.15 = (s32[]{:T(128)}, f32[32,512,256]{2,1,0:T(8,128)}, f32[16,512,256]{2,1,0:T(8,128)}, s32[16]{0:T(128)S(1)}, s32[]{:T(128)}, /*index=5*/s32[16,512,512]...) while((s32[]{:T(128)}, f32[32,512,256]{2,1,0:T(8,128)}, ...), condition=%wide.region_3.4_spmd, body=%wide.region_0.3_spmd.sunk | while | flops 1629497344 | bytes 35717552 | solution.py:52
  130.9 0.7 add_compare_fusion.2
  131.6 0.6 gather_fusion
  132.9 4.0 gather_fusion.2
  136.9 2.8 gather_fusion.3
  139.7 5.6 %select_convert_fusion.8 = bf16[4,512,512]{2,1,0:T(8,128)(2,1)S(1)} fusion(s32[16,512,512]{2,1,0:T(8,128)} %get-tuple-element.329, s32[]{:T(128)S(6)} %select_n.185, f32[4,512]{1,0:T(4,128)S(1)} %select_convert_fusion.6, f32[4,512]{1,0:T(4,128)S(1)} %select_convert_fusion.7, pred[4]{0:T(512)(128)(4,1)S(1)} %add_compare_fusion.2, ...), kind=kOutput, calls=%fused_computation.6.clone.1 | convolution fusion | flops 553648128 | bytes 8405008 | tf_op jit(solution)/shard_map/while/body/eval_jaxpr/sbd,sed->sbe/dot_general | solution.py:34
  145.3 2.2 fusion.18
  147.5 0.8 fusion.17
  148.3 4.9 %scatter_fusion.1 = f32[16,512,256]{2,1,0:T(8,128)} fusion(f32[16,512,256]{2,1,0:T(8,128)} %get-tuple-element.311, s32[4]{0:T(128)S(1)} %get-tuple-element.291, f32[4,512,256]{2,1,0:T(8,128)} %fusion.18), kind=kCustom, calls=%fused_computation.5.clone.1 | custom fusion | flops 524288 | bytes 6291472 | tf_op jit(solution)/shard_map/while/body/eval_jaxpr/scatter-add | solution.py:49
  153.2 4.3 %scatter_fusion = f32[32,512,256]{2,1,0:T(8,128)} fusion(f32[32,512,256]{2,1,0:T(8,128)} %get-tuple-element.310, s32[4]{0:T(128)S(1)} %get-tuple-element.290, f32[4,512,256]{2,1,0:T(8,128)S(1)} %fusion.17), kind=kCustom, calls=%fused_computation.4.clone.1 | custom fusion | flops 524288 | bytes 6291472 | tf_op jit(solution)/shard_map/while/body/eval_jaxpr/scatter-add | solution.py:49
  157.5 0.7 add_compare_fusion.2
  158.2 0.6 gather_fusion
  159.5 4.0 gather_fusion.2
  163.5 2.8 gather_fusion.3
  166.3 5.6 %select_convert_fusion.8 = bf16[4,512,512]{2,1,0:T(8,128)(2,1)S(1)} fusion(s32[16,512,512]{2,1,0:T(8,128)} %get-tuple-element.329, s32[]{:T(128)S(6)} %select_n.185, f32[4,512]{1,0:T(4,128)S(1)} %select_convert_fusion.6, f32[4,512]{1,0:T(4,128)S(1)} %select_convert_fusion.7, pred[4]{0:T(512)(128)(4,1)S(1)} %add_compare_fusion.2, ...), kind=kOutput, calls=%fused_computation.6.clone.1 | convolution fusion | flops 553648128 | bytes 8405008 | tf_op jit(solution)/shard_map/while/body/eval_jaxpr/sbd,sed->sbe/dot_general | solution.py:34
  171.9 2.2 fusion.18
  174.1 0.8 fusion.17
  174.9 5.0 %scatter_fusion.1 = f32[16,512,256]{2,1,0:T(8,128)} fusion(f32[16,512,256]{2,1,0:T(8,128)} %get-tuple-element.311, s32[4]{0:T(128)S(1)} %get-tuple-element.291, f32[4,512,256]{2,1,0:T(8,128)} %fusion.18), kind=kCustom, calls=%fused_computation.5.clone.1 | custom fusion | flops 524288 | bytes 6291472 | tf_op jit(solution)/shard_map/while/body/eval_jaxpr/scatter-add | solution.py:49
  179.9 4.2 %scatter_fusion = f32[32,512,256]{2,1,0:T(8,128)} fusion(f32[32,512,256]{2,1,0:T(8,128)} %get-tuple-element.310, s32[4]{0:T(128)S(1)} %get-tuple-element.290, f32[4,512,256]{2,1,0:T(8,128)S(1)} %fusion.17), kind=kCustom, calls=%fused_computation.4.clone.1 | custom fusion | flops 524288 | bytes 6291472 | tf_op jit(solution)/shard_map/while/body/eval_jaxpr/scatter-add | solution.py:49
  184.1 0.7 add_compare_fusion.2
  184.9 0.6 gather_fusion
  186.2 4.0 gather_fusion.2
  190.2 2.8 gather_fusion.3
  193.0 5.6 %select_convert_fusion.8 = bf16[4,512,512]{2,1,0:T(8,128)(2,1)S(1)} fusion(s32[16,512,512]{2,1,0:T(8,128)} %get-tuple-element.329, s32[]{:T(128)S(6)} %select_n.185, f32[4,512]{1,0:T(4,128)S(1)} %select_convert_fusion.6, f32[4,512]{1,0:T(4,128)S(1)} %select_convert_fusion.7, pred[4]{0:T(512)(128)(4,1)S(1)} %add_compare_fusion.2, ...), kind=kOutput, calls=%fused_computation.6.clone.1 | convolution fusion | flops 553648128 | bytes 8405008 | tf_op jit(solution)/shard_map/while/body/eval_jaxpr/sbd,sed->sbe/dot_general | solution.py:34
  198.6 2.2 fusion.18
  200.8 0.8 fusion.17
  201.6 5.1 %scatter_fusion.1 = f32[16,512,256]{2,1,0:T(8,128)} fusion(f32[16,512,256]{2,1,0:T(8,128)} %get-tuple-element.311, s32[4]{0:T(128)S(1)} %get-tuple-element.291, f32[4,512,256]{2,1,0:T(8,128)} %fusion.18), kind=kCustom, calls=%fused_computation.5.clone.1 | custom fusion | flops 524288 | bytes 6291472 | tf_op jit(solution)/shard_map/while/body/eval_jaxpr/scatter-add | solution.py:49
  206.6 4.3 %scatter_fusion = f32[32,512,256]{2,1,0:T(8,128)} fusion(f32[32,512,256]{2,1,0:T(8,128)} %get-tuple-element.310, s32[4]{0:T(128)S(1)} %get-tuple-element.290, f32[4,512,256]{2,1,0:T(8,128)S(1)} %fusion.17), kind=kCustom, calls=%fused_computation.4.clone.1 | custom fusion | flops 524288 | bytes 6291472 | tf_op jit(solution)/shard_map/while/body/eval_jaxpr/scatter-add | solution.py:49
  210.9 0.7 add_compare_fusion.2
  211.7 0.6 gather_fusion
  212.3 0.6 gather_fusion.1
  213.0 4.0 gather_fusion.2
  217.0 2.8 gather_fusion.3
  219.8 5.6 %select_convert_fusion.8 = bf16[4,512,512]{2,1,0:T(8,128)(2,1)S(1)} fusion(s32[16,512,512]{2,1,0:T(8,128)} %get-tuple-element.329, s32[]{:T(128)S(6)} %select_n.185, f32[4,512]{1,0:T(4,128)S(1)} %select_convert_fusion.6, f32[4,512]{1,0:T(4,128)S(1)} %select_convert_fusion.7, pred[4]{0:T(512)(128)(4,1)S(1)} %add_compare_fusion.2, ...), kind=kOutput, calls=%fused_computation.6.clone.1 | convolution fusion | flops 553648128 | bytes 8405008 | tf_op jit(solution)/shard_map/while/body/eval_jaxpr/sbd,sed->sbe/dot_general | solution.py:34
  225.3 2.2 fusion.18
  227.6 0.8 fusion.17
  228.4 5.0 %scatter_fusion.1 = f32[16,512,256]{2,1,0:T(8,128)} fusion(f32[16,512,256]{2,1,0:T(8,128)} %get-tuple-element.311, s32[4]{0:T(128)S(1)} %get-tuple-element.291, f32[4,512,256]{2,1,0:T(8,128)} %fusion.18), kind=kCustom, calls=%fused_computation.5.clone.1 | custom fusion | flops 524288 | bytes 6291472 | tf_op jit(solution)/shard_map/while/body/eval_jaxpr/scatter-add | solution.py:49
  233.4 4.2 %scatter_fusion = f32[32,512,256]{2,1,0:T(8,128)} fusion(f32[32,512,256]{2,1,0:T(8,128)} %get-tuple-element.310, s32[4]{0:T(128)S(1)} %get-tuple-element.290, f32[4,512,256]{2,1,0:T(8,128)S(1)} %fusion.17), kind=kCustom, calls=%fused_computation.4.clone.1 | custom fusion | flops 524288 | bytes 6291472 | tf_op jit(solution)/shard_map/while/body/eval_jaxpr/scatter-add | solution.py:49
  238.2 51.0 %reduce-scatter.5.cloned.1.call-done = f32[1024,256]{1,0:T(8,128)} async-done(((f32[8192,256]{1,0:T(8,128)}), f32[1024,256]{1,0:T(8,128)}) %reduce-scatter.5.cloned.1.call-update) | async-done | bytes 1048592 | tf_op jit(solution)/shard_map/reduce_scatter | solution.py:105
  289.2 2.4 multiply_subtract_fusion
  291.6 111.7 %reduce-scatter.3.cloned.1.call-done = f32[1024,256]{1,0:T(8,128)} async-done(((f32[16384,256]{1,0:T(8,128)}), f32[1024,256]{1,0:T(8,128)}) %reduce-scatter.3.cloned.1.call-update) | async-done | bytes 1048592 | tf_op jit(solution)/shard_map/reduce_scatter | solution.py:102
  403.2 2.7 multiply_subtract_fusion.1
  (96 shorter events, 3.9 us)
Async XLA Ops:
  7.2 4.4 %copy-start.3 = (bf16[1024]{0:T(1024)(128)(2,1)S(1)}, bf16[1024]{0:T(1024)(128)(2,1)}, u32[]{:S(2)}) copy-start(bf16[1024]{0:T(1024)(128)(2,1)} %param.18) | copy-start | bytes 6148
  7.2 41.0 %copy-start.6 = (s32[16]{0:T(128)S(1)}, s32[16]{0:T(128)}, u32[]{:S(2)}) copy-start(s32[16]{0:T(128)} %param.14) | copy-start | bytes 196
  7.2 41.0 %copy-start.5 = (s32[16]{0:T(128)S(1)}, s32[16]{0:T(128)}, u32[]{:S(2)}) copy-start(s32[16]{0:T(128)} %param.13) | copy-start | bytes 196
  7.2 46.7 %copy-start.4 = (bf16[1024]{0:T(1024)(128)(2,1)S(1)}, bf16[1024]{0:T(1024)(128)(2,1)}, u32[]{:S(2)}) copy-start(bf16[1024]{0:T(1024)(128)(2,1)} %param.21) | copy-start | bytes 6148
  7.2 73.5 %all-gather.5.cloned.1.call-start = ((), (), s32[]{:S(2)}) async-start(), calls=%async_computation.3 | async-start | bytes 4718592 | tf_op jit(solution)/shard_map/all_gather | solution.py:77
  9.3 109.7 %all-gather.3.cloned.1.call-start = ((), (), s32[]{:S(2)}) async-start(), calls=%async_computation.2 | async-start | bytes 8912896 | tf_op jit(solution)/shard_map/all_gather | solution.py:79
  11.5 277.7 %reduce-scatter.5.cloned.1.call-start = ((), (), s32[]{:S(2)}) async-start(), calls=%async_computation.5 | async-start | bytes 9437184 | tf_op jit(solution)/shard_map/reduce_scatter | solution.py:105
  11.6 7.8 %collective-permute-start = (bf16[1024]{0:T(1024)(128)(2,1)S(1)}, bf16[1024]{0:T(1024)(128)(2,1)S(1)}, u32[]{:S(2)}, u32[]{:S(2)}) collective-permute-start(bf16[1024]{0:T(1024)(128)(2,1)S(1)} %copy-done.3), channel_id=1, source_target_pairs={{0,8},{8,16},{16,24},{24,32},{32,40},{40,48},{48,56},{56,64},{64,7... | collective-permute-start | bytes 6152 | tf_op jit(solution)/shard_map/ppermute | solution.py:85
  19.4 5.8 %collective-permute-start.1 = (bf16[1024]{0:T(1024)(128)(2,1)S(1)}, bf16[1024]{0:T(1024)(128)(2,1)S(1)}, u32[]{:S(2)}, u32[]{:S(2)}) collective-permute-start(bf16[1024]{0:T(1024)(128)(2,1)S(1)} %collective-permute-done), channel_id=1, source_target_pairs={{0,8},{8,16},{16,24},{24,32},{32,40},{40,48},{48,56},{56,64},{64,7... | collective-permute-start | bytes 6152 | tf_op jit(solution)/shard_map/ppermute | solution.py:85
  19.4 5.8 %collective-permute-start.8 = (bf16[1024]{0:T(1024)(128)(2,1)S(1)}, bf16[1024]{0:T(1024)(128)(2,1)S(1)}, u32[]{:S(2)}, u32[]{:S(2)}) collective-permute-start(bf16[1024]{0:T(1024)(128)(2,1)S(1)} %copy-done.3), channel_id=1, source_target_pairs={{0,120},{8,0},{16,8},{24,16},{32,24},{40,32},{48,40},{56,48},{64,5... | collective-permute-start | bytes 6152 | tf_op jit(solution)/shard_map/ppermute | solution.py:87
  25.1 5.8 %collective-permute-start.2 = (bf16[1024]{0:T(1024)(128)(2,1)S(1)}, bf16[1024]{0:T(1024)(128)(2,1)S(1)}, u32[]{:S(2)}, u32[]{:S(2)}) collective-permute-start(bf16[1024]{0:T(1024)(128)(2,1)S(1)} %collective-permute-done.1), channel_id=1, source_target_pairs={{0,8},{8,16},{16,24},{24,32},{32,40},{40,48},{48,56},{56,64},{64,7... | collective-permute-start | bytes 6152 | tf_op jit(solution)/shard_map/ppermute | solution.py:85
  25.1 5.8 %collective-permute-start.9 = (bf16[1024]{0:T(1024)(128)(2,1)S(1)}, bf16[1024]{0:T(1024)(128)(2,1)S(1)}, u32[]{:S(2)}, u32[]{:S(2)}) collective-permute-start(bf16[1024]{0:T(1024)(128)(2,1)S(1)} %collective-permute-done.8), channel_id=1, source_target_pairs={{0,120},{8,0},{16,8},{24,16},{32,24},{40,32},{48,40},{56,48},{64,5... | collective-permute-start | bytes 6152 | tf_op jit(solution)/shard_map/ppermute | solution.py:87
  30.9 5.8 %collective-permute-start.3 = (bf16[1024]{0:T(1024)(128)(2,1)S(1)}, bf16[1024]{0:T(1024)(128)(2,1)S(1)}, u32[]{:S(2)}, u32[]{:S(2)}) collective-permute-start(bf16[1024]{0:T(1024)(128)(2,1)S(1)} %collective-permute-done.2), channel_id=1, source_target_pairs={{0,8},{8,16},{16,24},{24,32},{32,40},{40,48},{48,56},{56,64},{64,7... | collective-permute-start | bytes 6152 | tf_op jit(solution)/shard_map/ppermute | solution.py:85
  30.9 5.8 %collective-permute-start.10 = (bf16[1024]{0:T(1024)(128)(2,1)S(1)}, bf16[1024]{0:T(1024)(128)(2,1)S(1)}, u32[]{:S(2)}, u32[]{:S(2)}) collective-permute-start(bf16[1024]{0:T(1024)(128)(2,1)S(1)} %collective-permute-done.9), channel_id=1, source_target_pairs={{0,120},{8,0},{16,8},{24,16},{32,24},{40,32},{48,40},{56,48},{64,5... | collective-permute-start | bytes 6152 | tf_op jit(solution)/shard_map/ppermute | solution.py:87
  36.6 5.8 %collective-permute-start.4 = (bf16[1024]{0:T(1024)(128)(2,1)S(1)}, bf16[1024]{0:T(1024)(128)(2,1)S(1)}, u32[]{:S(2)}, u32[]{:S(2)}) collective-permute-start(bf16[1024]{0:T(1024)(128)(2,1)S(1)} %collective-permute-done.3), channel_id=1, source_target_pairs={{0,8},{8,16},{16,24},{24,32},{32,40},{40,48},{48,56},{56,64},{64,7... | collective-permute-start | bytes 6152 | tf_op jit(solution)/shard_map/ppermute | solution.py:85
  36.6 5.8 %collective-permute-start.11 = (bf16[1024]{0:T(1024)(128)(2,1)S(1)}, bf16[1024]{0:T(1024)(128)(2,1)S(1)}, u32[]{:S(2)}, u32[]{:S(2)}) collective-permute-start(bf16[1024]{0:T(1024)(128)(2,1)S(1)} %collective-permute-done.10), channel_id=1, source_target_pairs={{0,120},{8,0},{16,8},{24,16},{32,24},{40,32},{48,40},{56,48},{64,5... | collective-permute-start | bytes 6152 | tf_op jit(solution)/shard_map/ppermute | solution.py:87
  42.4 5.8 %collective-permute-start.5 = (bf16[1024]{0:T(1024)(128)(2,1)S(1)}, bf16[1024]{0:T(1024)(128)(2,1)S(1)}, u32[]{:S(2)}, u32[]{:S(2)}) collective-permute-start(bf16[1024]{0:T(1024)(128)(2,1)S(1)} %collective-permute-done.4), channel_id=1, source_target_pairs={{0,8},{8,16},{16,24},{24,32},{32,40},{40,48},{48,56},{56,64},{64,7... | collective-permute-start | bytes 6152 | tf_op jit(solution)/shard_map/ppermute | solution.py:85
  42.4 5.8 %collective-permute-start.12 = (bf16[1024]{0:T(1024)(128)(2,1)S(1)}, bf16[1024]{0:T(1024)(128)(2,1)S(1)}, u32[]{:S(2)}, u32[]{:S(2)}) collective-permute-start(bf16[1024]{0:T(1024)(128)(2,1)S(1)} %collective-permute-done.11), channel_id=1, source_target_pairs={{0,120},{8,0},{16,8},{24,16},{32,24},{40,32},{48,40},{56,48},{64,5... | collective-permute-start | bytes 6152 | tf_op jit(solution)/shard_map/ppermute | solution.py:87
  48.1 5.8 %collective-permute-start.6 = (bf16[1024]{0:T(1024)(128)(2,1)S(1)}, bf16[1024]{0:T(1024)(128)(2,1)S(1)}, u32[]{:S(2)}, u32[]{:S(2)}) collective-permute-start(bf16[1024]{0:T(1024)(128)(2,1)S(1)} %collective-permute-done.5), channel_id=1, source_target_pairs={{0,8},{8,16},{16,24},{24,32},{32,40},{40,48},{48,56},{56,64},{64,7... | collective-permute-start | bytes 6152 | tf_op jit(solution)/shard_map/ppermute | solution.py:85
  48.2 26.2 %collective-permute-start.13 = (bf16[1024]{0:T(1024)(128)(2,1)S(1)}, bf16[1024]{0:T(1024)(128)(2,1)S(1)}, u32[]{:S(2)}, u32[]{:S(2)}) collective-permute-start(bf16[1024]{0:T(1024)(128)(2,1)S(1)} %collective-permute-done.12), channel_id=1, source_target_pairs={{0,120},{8,0},{16,8},{24,16},{32,24},{40,32},{48,40},{56,48},{64,5... | collective-permute-start | bytes 6152 | tf_op jit(solution)/shard_map/ppermute | solution.py:87
  53.9 25.8 %collective-permute-start.7 = (bf16[1024]{0:T(1024)(128)(2,1)S(1)}, bf16[1024]{0:T(1024)(128)(2,1)S(1)}, u32[]{:S(2)}, u32[]{:S(2)}) collective-permute-start(bf16[1024]{0:T(1024)(128)(2,1)S(1)} %collective-permute-done.6), channel_id=1, source_target_pairs={{0,8},{8,16},{16,24},{24,32},{32,40},{40,48},{48,56},{56,64},{64,7... | collective-permute-start | bytes 6152 | tf_op jit(solution)/shard_map/ppermute | solution.py:85
  74.4 6.0 %collective-permute-start.14 = (bf16[1024]{0:T(1024)(128)(2,1)S(1)}, bf16[1024]{0:T(1024)(128)(2,1)S(1)}, u32[]{:S(2)}, u32[]{:S(2)}) collective-permute-start(bf16[1024]{0:T(1024)(128)(2,1)S(1)} %collective-permute-done.13), channel_id=1, source_target_pairs={{0,120},{8,0},{16,8},{24,16},{32,24},{40,32},{48,40},{56,48},{64,5... | collective-permute-start | bytes 6152 | tf_op jit(solution)/shard_map/ppermute | solution.py:87
  237.6 165.6 %reduce-scatter.3.cloned.1.call-start = ((), (), s32[]{:S(2)}) async-start(), calls=%async_computation.4 | async-start | bytes 17825792 | tf_op jit(solution)/shard_map/reduce_scatter | solution.py:102
  237.7 51.5 %copy-start = (f32[1024,256]{1,0:T(8,128)S(1)}, f32[1024,256]{1,0:T(8,128)}, u32[]{:S(2)}) copy-start(f32[1024,256]{1,0:T(8,128)} %param.19) | copy-start | bytes 3145732
  237.7 51.5 %copy-start.2 = (f32[1024,256]{1,0:T(8,128)S(1)}, f32[1024,256]{1,0:T(8,128)}, u32[]{:S(2)}) copy-start(f32[1024,256]{1,0:T(8,128)} %param.20) | copy-start | bytes 3145732
  238.2 165.0 %copy-start.1 = (f32[1024,256]{1,0:T(8,128)S(1)}, f32[1024,256]{1,0:T(8,128)}, u32[]{:S(2)}) copy-start(f32[1024,256]{1,0:T(8,128)} %param.16) | copy-start | bytes 3145732
Sparse Core Ops, SparseCore 0:
  10.3 35.6 all-gather.4
  48.7 70.2 all-gather.2
  237.7 51.3 reduce-scatter.4
  292.4 110.7 reduce-scatter.2
